TPU v7x, 32 devices: a whole 2x2x4 slice. The times are simulated.
32 devices in a mesh: shard: 4 (over y, core), rep: 8 (over z, x).
Axes of the slice: x: 2, y: 2, z: 4, core: 2. Of those that a mesh axis runs over, the one named last changes fastest.
Arguments:
- block_input: bfloat16 [4096, 1024], P(('shard', 'rep')), may hold values from -6 to 6
- segments: int32 [4096], P(('shard', 'rep')), may hold values from 0 to 95, never falling along the last dimension, each value on 1 to 96 neighbouring positions
- cotangent: bfloat16 [4096, 1024], P(('shard', 'rep')), may hold values from -6 to 6
- gain_in: float32 [1024], replicated, may hold values from 0.5 to 1.5
- w_query: bfloat16 [1024, 768], P('shard'), may hold values from -0.1875 to 0.1875
- w_key: bfloat16 [1024, 768], P('shard'), may hold values from -0.1875 to 0.1875
- w_value: bfloat16 [1024, 1536], P('shard'), may hold values from -0.1875 to 0.1875
- conv_q: float32 [4, 768], replicated, may hold values from -3 to 3
- conv_k: float32 [4, 768], replicated, may hold values from -3 to 3
- conv_v: float32 [4, 1536], replicated, may hold values from -3 to 3
- w_decay: bfloat16 [1024, 6], replicated, may hold values from -0.1875 to 0.1875
- w_beta: bfloat16 [1024, 6], replicated, may hold values from -0.1875 to 0.1875
- a_log: float32 [6], replicated, may hold values from -3 to 0.5
- dt_bias: float32 [6], replicated, may hold values from -3 to -1
- w_gate_out: bfloat16 [1024, 1536], P('shard'), may hold values from -0.1875 to 0.1875
- gain_o: float32 [256], replicated, may hold values from 0.5 to 1.5
- w_out: bfloat16 [1536, 1024], P('shard'), may hold values from -0.3125 to 0.3125
- gain_mid: float32 [1024], replicated, may hold values from 0.5 to 1.5
- w_ffgate: bfloat16 [1024, 2816], P('shard'), may hold values from -0.1875 to 0.1875
- w_ffup: bfloat16 [1024, 2816], P('shard'), may hold values from -0.1875 to 0.1875
- w_down: bfloat16 [2816, 1024], P('shard'), may hold values from -0.21875 to 0.21875
Outputs:
- block_output: bfloat16 [4096, 1024], P(('shard', 'rep'))
- d_input: float32 [4096, 1024], P(('shard', 'rep'))
- d_gain_in: float32 [1024], replicated
- d_query: float32 [1024, 768], P('shard', 'rep')
- d_key: float32 [1024, 768], P('shard', 'rep')
- d_value: float32 [1024, 1536], P('shard', 'rep')
- d_conv_q: float32 [4, 768], replicated
- d_conv_k: float32 [4, 768], replicated
- d_conv_v: float32 [4, 1536], replicated
- d_decay: float32 [1024, 6], replicated
- d_beta: float32 [1024, 6], replicated
- d_a_log: float32 [6], replicated
- d_dt_bias: float32 [6], replicated
- d_gate_out: float32 [1024, 1536], P('shard', 'rep')
- d_gain_o: float32 [256], replicated
- d_out: float32 [1536, 1024], P('shard', 'rep')
- d_gain_mid: float32 [1024], replicated
- d_ffgate: float32 [1024, 2816], P('shard', 'rep')
- d_ffup: float32 [1024, 2816], P('shard', 'rep')
- d_down: float32 [2816, 1024], P('shard', 'rep')
Inputs may be any that keep to these rules, and one draw needn't show every extreme that they name: `segments`: document numbers never fall along the tokens; a document covers 1 to (96) tokens, and one covers exactly that many.
All inputs are finite; a program needn't handle non-finite values.
Results may differ from a plain program's by a relative error of at most 0.017.
The roundings to bfloat16 on the way count: a program that leaves them out, or rounds other values in their place, can miss the bound.
Values may be sent and summed in bfloat16 or wider, within the bound.
No kernel may reach another device: no remote copies, remote signals or barrier semaphores. Data moves between devices by JAX's collectives and lax.ppermute only.
A program may use at most 192 MiB of HBM per device.

v0:
```python
from functools import partial
import jax
import jax.numpy as jnp
from jax import lax
from jax.sharding import PartitionSpec as P

SPAN = 64
SEQ = 128


def norm_apply(hidden, gain):
    return hidden * lax.rsqrt(jnp.mean(hidden * hidden, axis=-1, keepdims=True) + 1e-05) * gain


def causal_conv(stream, taps, same_list):
    total = stream * taps[0]
    for lag in range(1, taps.shape[0]):
        moved = jnp.pad(stream, ((0, 0), (lag, 0), (0, 0)))[:, : stream.shape[1]]
        total = total + moved * taps[lag] * same_list[lag][:, :, None]
    return jax.nn.silu(total)


def unit_heads(stream, heads):
    batch, length, width = stream.shape
    split = stream.reshape(batch, length, heads, width // heads)
    return split * lax.rsqrt(jnp.sum(split * split, axis=-1, keepdims=True) + 1e-06)


def to_blocks(array, batch, blocks):
    shaped = array.reshape((batch, blocks, SPAN) + array.shape[2:])
    return jnp.moveaxis(jnp.moveaxis(shaped, 1, 0), 2, 3)


def mixer(seg, qp, kp, vp, zp, decay_raw, beta_raw, conv_q, conv_k, conv_v, a_log, dt_bias, gain_o):
    batch, length = seg.shape
    heads = a_log.shape[0]
    highest = lax.Precision.HIGHEST
    same_list = []
    for lag in range(conv_q.shape[0]):
        earlier = jnp.pad(seg, ((0, 0), (lag, 0)), constant_values=-1)[:, :length]
        same_list.append((earlier == seg).astype(jnp.float32))
    query = unit_heads(causal_conv(qp, conv_q, same_list), heads)
    query = query * query.shape[-1] ** (-0.5)
    keys = unit_heads(causal_conv(kp, conv_k, same_list), heads)
    value = causal_conv(vp, conv_v, same_list)
    value = value.reshape(batch, length, heads, value.shape[-1] // heads)
    log_decay = -jnp.exp(a_log) * jax.nn.softplus(decay_raw + dt_bias)
    beta = jax.nn.sigmoid(beta_raw)
    blocks = length // SPAN
    query_b = to_blocks(query, batch, blocks)
    keys_b = to_blocks(keys, batch, blocks)
    value_b = to_blocks(value, batch, blocks)
    decay_b = to_blocks(log_decay, batch, blocks)
    beta_b = to_blocks(beta, batch, blocks)
    seg_b = jnp.moveaxis(seg.reshape(batch, blocks, SPAN), 1, 0)
    seg_prev = jnp.concatenate([jnp.full((1, batch), -1, seg.dtype), seg_b[:-1, :, -1]], axis=0)
    identity = jnp.eye(SPAN, dtype=jnp.float32)
    lower = jnp.tril(jnp.ones((SPAN, SPAN), jnp.float32))
    width_v = value.shape[-1]

    def span_step(state, items):
        qc, kc, vc, gc, bc, sc, sp = items
        cum = jnp.cumsum(gc, axis=-1)
        same = (sc[:, :, None] == sc[:, None, :]).astype(jnp.float32) * lower
        decay = jnp.exp(jnp.minimum(cum[..., :, None] - cum[..., None, :], 0.0)) * same[:, None]
        enter = jnp.exp(cum) * (sc == sp[:, None]).astype(jnp.float32)[:, None, :]
        inner = jnp.einsum("bhtd,bhsd->bhts", kc, kc, precision=highest)
        system = identity + bc[..., :, None] * decay * (1.0 - identity) * inner
        rhs = jnp.concatenate([bc[..., None] * vc, (bc * enter)[..., None] * kc], axis=-1)
        solved = jax.scipy.linalg.solve_triangular(system, rhs, lower=True, unit_diagonal=True)
        fresh = solved[..., :width_v] - jnp.einsum(
            "bhtk,bhkv->bhtv", solved[..., width_v:], state, precision=highest
        )
        scores = jnp.einsum("bhtd,bhsd->bhts", qc, kc, precision=highest) * decay
        result = enter[..., None] * jnp.einsum("bhtk,bhkv->bhtv", qc, state, precision=highest)
        result = result + jnp.einsum("bhts,bhsv->bhtv", scores, fresh, precision=highest)
        weighted = decay[..., -1, :][..., None] * kc
        new_state = enter[..., -1][..., None, None] * state + jnp.einsum(
            "bhsk,bhsv->bhkv", weighted, fresh, precision=highest
        )
        return (new_state, result)

    start = jnp.zeros((batch, heads, keys.shape[-1], width_v), jnp.float32)
    _, outs = lax.scan(
        span_step, start, (query_b, keys_b, value_b, decay_b, beta_b, seg_b, seg_prev)
    )
    core = jnp.moveaxis(jnp.moveaxis(outs, 3, 2), 0, 1).reshape(batch, length, heads, width_v)
    gated = core * lax.rsqrt(jnp.mean(core * core, axis=-1, keepdims=True) + 1e-05) * gain_o
    gated = gated * jax.nn.silu(zp.reshape(batch, length, heads, width_v))
    return gated.reshape(batch, length, heads * width_v)


def dot_plain(left, right):
    return jnp.dot(left, right, preferred_element_type=jnp.float32)


def dot_trans(left, right):
    return lax.dot_general(
        left, right, (((1,), (1,)), ((), ())), preferred_element_type=jnp.float32
    )


def dot_outer(left, right):
    return lax.dot_general(
        left, right, (((0,), (0,)), ((), ())), preferred_element_type=jnp.float32
    )


def keep_pair(left, right):
    return (left, right)


def forward_pass(tokens_in, segments, large, small):
    w_query, w_key, w_value, w_gate_out, w_out, w_ffgate, w_ffup, w_down = large
    gain_in, gain_mid, conv_q, conv_k, conv_v, w_decay, w_beta, a_log, dt_bias, gain_o = small
    rows = tokens_in.shape[0]
    batch = rows // SEQ
    seg = segments.reshape(batch, SEQ)
    resid = tokens_in.astype(jnp.float32)
    normed = norm_apply(resid, gain_in).astype(jnp.bfloat16)
    inputs = tuple(
        (
            dot_plain(normed, weight)
            for weight in (w_query, w_key, w_value, w_gate_out, w_decay, w_beta)
        )
    )
    shaped = tuple((item.reshape(batch, SEQ, item.shape[-1]) for item in inputs))
    mixed = (
        mixer(seg, *shaped, conv_q, conv_k, conv_v, a_log, dt_bias, gain_o)
        .reshape(rows, -1)
        .astype(jnp.bfloat16)
    )
    hidden1 = resid + dot_plain(mixed, w_out)
    normed2 = norm_apply(hidden1, gain_mid).astype(jnp.bfloat16)
    gate = dot_plain(normed2, w_ffgate)
    up = dot_plain(normed2, w_ffup)
    act = (jax.nn.silu(gate) * up).astype(jnp.bfloat16)
    output = (hidden1 + dot_plain(act, w_down)).astype(jnp.bfloat16)
    saved = (resid, normed, shaped, seg, mixed, hidden1, normed2, gate, up, act)
    return (saved, output)


def backward_ffn(saved, cotangent, large, small, outer):
    resid, normed, shaped, seg, mixed, hidden1, normed2, gate, up, act = saved
    w_ffgate, w_ffup, w_down = (large[5], large[6], large[7])
    gain_mid = small[1]
    g_down = outer(act, cotangent)
    d_act = dot_trans(cotangent, w_down)
    sig = jax.nn.sigmoid(gate)
    d_gate = (d_act * up * sig * (1.0 + gate * (1.0 - sig))).astype(jnp.bfloat16)
    d_up = (d_act * gate * sig).astype(jnp.bfloat16)
    g_ffgate = outer(normed2, d_gate)
    g_ffup = outer(normed2, d_up)
    d_normed2 = dot_trans(d_gate, w_ffgate) + dot_trans(d_up, w_ffup)
    _, pull = jax.vjp(norm_apply, hidden1, gain_mid)
    d_from_norm, g_gain_mid = pull(d_normed2)
    d_hidden1 = cotangent.astype(jnp.float32) + d_from_norm
    return (d_hidden1, (g_ffgate, g_ffup, g_down), g_gain_mid)


def backward_mixer(saved, d_hidden1, large, small, outer):
    resid, normed, shaped, seg, mixed, hidden1, normed2, gate, up, act = saved
    w_query, w_key, w_value, w_gate_out, w_out = large[:5]
    gain_in, gain_mid, conv_q, conv_k, conv_v, w_decay, w_beta, a_log, dt_bias, gain_o = small
    rows = resid.shape[0]
    d_hidden_b = d_hidden1.astype(jnp.bfloat16)
    g_out = outer(mixed, d_hidden_b)
    d_mixed = dot_trans(d_hidden_b, w_out)
    _, pull = jax.vjp(partial(mixer, seg), *shaped, conv_q, conv_k, conv_v, a_log, dt_bias, gain_o)
    grads = pull(d_mixed.reshape(shaped[2].shape[0], SEQ, -1))
    flat = tuple((item.reshape(rows, -1).astype(jnp.bfloat16) for item in grads[:6]))
    weights = (w_query, w_key, w_value, w_gate_out, w_decay, w_beta)
    g_proj = tuple((outer(normed, item) for item in flat[:4]))
    g_decay = dot_outer(normed, flat[4])
    g_beta = dot_outer(normed, flat[5])
    d_normed = dot_trans(flat[0], weights[0])
    for item, weight in zip(flat[1:], weights[1:]):
        d_normed = d_normed + dot_trans(item, weight)
    _, pull_in = jax.vjp(norm_apply, resid, gain_in)
    d_from_norm, g_gain_in = pull_in(d_normed)
    d_input = d_hidden1 + d_from_norm
    large_grads = (g_proj[0], g_proj[1], g_proj[2], g_proj[3], g_out)
    small_grads = (
        g_gain_in,
        grads[6],
        grads[7],
        grads[8],
        g_decay,
        g_beta,
        grads[9],
        grads[10],
        grads[11],
    )
    return (d_input, large_grads, small_grads)


def owned_columns(left, count, index):
    width = left.shape[1] // count
    return lax.dynamic_slice_in_dim(left, index * width, width, 1)


def body(
    block_input,
    segments,
    cotangent,
    gain_in,
    w_query,
    w_key,
    w_value,
    conv_q,
    conv_k,
    conv_v,
    w_decay,
    w_beta,
    a_log,
    dt_bias,
    w_gate_out,
    gain_o,
    w_out,
    gain_mid,
    w_ffgate,
    w_ffup,
    w_down,
):
    small = (gain_in, gain_mid, conv_q, conv_k, conv_v, w_decay, w_beta, a_log, dt_bias, gain_o)
    gathered = (
        lax.all_gather(w_query, "shard", axis=0, tiled=True),
        lax.all_gather(w_key, "shard", axis=0, tiled=True),
        lax.all_gather(w_value, "shard", axis=0, tiled=True),
        lax.all_gather(w_gate_out, "shard", axis=0, tiled=True),
        lax.all_gather(w_out, "shard", axis=0, tiled=True),
        lax.all_gather(w_ffgate, "shard", axis=0, tiled=True),
        lax.all_gather(w_ffup, "shard", axis=0, tiled=True),
        lax.all_gather(w_down, "shard", axis=0, tiled=True),
    )
    saved, output = forward_pass(block_input, segments, gathered, small)
    d_hidden1, ffn_pairs, g_gain_mid = backward_ffn(saved, cotangent, gathered, small, keep_pair)
    d_input, mix_pairs, mix_small = backward_mixer(saved, d_hidden1, gathered, small, keep_pair)
    factors = (
        lax.all_gather(mix_pairs[0][0], "shard", axis=0, tiled=True),
        lax.all_gather(mix_pairs[4][0], "shard", axis=0, tiled=True),
        lax.all_gather(ffn_pairs[0][0], "shard", axis=0, tiled=True),
        lax.all_gather(ffn_pairs[2][0], "shard", axis=0, tiled=True),
        lax.all_gather(mix_pairs[0][1], "shard", axis=0, tiled=True),
        lax.all_gather(mix_pairs[1][1], "shard", axis=0, tiled=True),
        lax.all_gather(mix_pairs[2][1], "shard", axis=0, tiled=True),
        lax.all_gather(mix_pairs[3][1], "shard", axis=0, tiled=True),
        lax.all_gather(mix_pairs[4][1], "shard", axis=0, tiled=True),
        lax.all_gather(ffn_pairs[0][1], "shard", axis=0, tiled=True),
        lax.all_gather(ffn_pairs[1][1], "shard", axis=0, tiled=True),
        lax.all_gather(ffn_pairs[2][1], "shard", axis=0, tiled=True),
    )
    count = lax.axis_size("shard")
    index = lax.axis_index("shard")
    normed_own = owned_columns(factors[0], count, index)
    mixed_own = owned_columns(factors[1], count, index)
    normed2_own = owned_columns(factors[2], count, index)
    act_own = owned_columns(factors[3], count, index)
    own_rows = (
        dot_outer(normed_own, factors[4]),
        dot_outer(normed_own, factors[5]),
        dot_outer(normed_own, factors[6]),
        dot_outer(normed_own, factors[7]),
        dot_outer(mixed_own, factors[8]),
        dot_outer(normed2_own, factors[9]),
        dot_outer(normed2_own, factors[10]),
        dot_outer(act_own, factors[11]),
    )
    large_final = (
        lax.psum_scatter(own_rows[0], "rep", scatter_dimension=1, tiled=True),
        lax.psum_scatter(own_rows[1], "rep", scatter_dimension=1, tiled=True),
        lax.psum_scatter(own_rows[2], "rep", scatter_dimension=1, tiled=True),
        lax.psum_scatter(own_rows[3], "rep", scatter_dimension=1, tiled=True),
        lax.psum_scatter(own_rows[4], "rep", scatter_dimension=1, tiled=True),
        lax.psum_scatter(own_rows[5], "rep", scatter_dimension=1, tiled=True),
        lax.psum_scatter(own_rows[6], "rep", scatter_dimension=1, tiled=True),
        lax.psum_scatter(own_rows[7], "rep", scatter_dimension=1, tiled=True),
    )
    small_terms = (mix_small[0], g_gain_mid) + tuple(mix_small[1:])
    small_final = lax.psum(
        (
            small_terms[0],
            small_terms[1],
            small_terms[2],
            small_terms[3],
            small_terms[4],
            small_terms[5],
            small_terms[6],
            small_terms[7],
            small_terms[8],
            small_terms[9],
        ),
        ("shard", "rep"),
    )
    g_query, g_key, g_value, g_gate_out, g_out, g_ffgate, g_ffup, g_down = large_final
    (
        g_gain_in,
        g_gain_mid2,
        g_conv_q,
        g_conv_k,
        g_conv_v,
        g_decay,
        g_beta,
        g_a_log,
        g_dt_bias,
        g_gain_o,
    ) = small_final
    return (
        output,
        d_input,
        g_gain_in,
        g_query,
        g_key,
        g_value,
        g_conv_q,
        g_conv_k,
        g_conv_v,
        g_decay,
        g_beta,
        g_a_log,
        g_dt_bias,
        g_gate_out,
        g_gain_o,
        g_out,
        g_gain_mid2,
        g_ffgate,
        g_ffup,
        g_down,
    )


def solution(mesh):
    return jax.shard_map(
        body,
        mesh=mesh,
        in_specs=(
            P(("shard", "rep"), None),
            P(("shard", "rep")),
            P(("shard", "rep"), None),
            P(),
            P("shard", None),
            P("shard", None),
            P("shard", None),
            P(),
            P(),
            P(),
            P(),
            P(),
            P(),
            P(),
            P("shard", None),
            P(),
            P("shard", None),
            P(),
            P("shard", None),
            P("shard", None),
            P("shard", None),
        ),
        out_specs=(
            P(("shard", "rep"), None),
            P(("shard", "rep"), None),
            P(),
            P("shard", "rep"),
            P("shard", "rep"),
            P("shard", "rep"),
            P(),
            P(),
            P(),
            P(),
            P(),
            P(),
            P(),
            P("shard", "rep"),
            P(),
            P("shard", "rep"),
            P(),
            P("shard", "rep"),
            P("shard", "rep"),
            P("shard", "rep"),
        ),
        check_vma=False,
    )
```

profile of v0, /device:TPU:0, one launch (start us, length us, event | category | flops | bytes accessed | tf_op | source)
XLA Modules:
  0.0 1416.3 jit_solution(15208728799947843738)
XLA Ops:
  22.7 9.3 all-gather.26.cloned.1.call-done
  33.9 19.4 %all-gather.22.cloned.1.call-done = bf16[1024,768]{1,0:T(8,128)(2,1)} async-done(((bf16[256,768]{1,0:T(8,128)(2,1)}), bf16[1024,768]{1,0:T(8,128)(2,1)}) %all-gather.22.cloned.1.call-update) | async-done | bytes 1572880 | tf_op jit(solution)/shard_map/all_gather | solution.py:228
  66.4 17.0 %all-gather.24.cloned.1.call-done = bf16[1024,1536]{1,0:T(8,128)(2,1)} async-done(((bf16[256,1536]{1,0:T(8,128)(2,1)}), bf16[1024,1536]{1,0:T(8,128)(2,1)}) %all-gather.24.cloned.1.call-update) | async-done | bytes 3145744 | tf_op jit(solution)/shard_map/all_gather | solution.py:229
  93.5 101.3 %while.103 = (s32[]{:T(128)}, f32[1,6,128,256]{3,2,1,0:T(8,128)S(1)}, f32[2,1,6,64,256]{4,3,2,1,0:T(8,128)}, f32[2,1,6,64]{3,2,1,0:T(8,128)}, s32[2,1,64]{2,1,0:...) while((s32[]{:T(128)}, ...), condition=%wide.region_5.7_spmd.clone.clone, body=%wide.region_3.6_spmd.clone.clone.sunk | while | flops 719243328 | bytes 16660529 | solution.py:84
  100.9 30.2 %custom-call.45 = f32[6,1,64,64]{2,3,1,0:T(8,128)S(1)} custom-call(f32[6,1,64,64]{3,2,1,0:T(8,128)} %fusion.510), custom_call_target="InvertDiagBlocksLowerTriangular" | custom-call | tf_op jit(solution)/shard_map/while/body/eval_jaxpr/jit(_solve_triangular)/vmap()/triangular_solve/custom-call.1 | solution.py:70
  151.5 30.2 %custom-call.45 = f32[6,1,64,64]{2,3,1,0:T(8,128)S(1)} custom-call(f32[6,1,64,64]{3,2,1,0:T(8,128)} %fusion.510), custom_call_target="InvertDiagBlocksLowerTriangular" | custom-call | tf_op jit(solution)/shard_map/while/body/eval_jaxpr/jit(_solve_triangular)/vmap()/triangular_solve/custom-call.1 | solution.py:70
  200.6 116.1 %while.104 = (s32[]{:T(128)}, f32[1,6,128,256]{3,2,1,0:T(8,128)S(1)}, f32[2,1,6,64,256]{4,3,2,1,0:T(8,128)}, f32[2,1,6,64,64]{4,3,2,1,0:T(8,128)}, f32[2,1,6,64,...) while((s32[]{:T(128)}, ...), condition=%wide.region_11.13_spmd.clone.clone, body=%wide.region_9.12_spmd.clone.clone.sunk | while | flops 719999424 | bytes 37368836 | solution.py:84
  208.5 30.1 %custom-call.46 = f32[6,1,64,64]{2,3,1,0:T(8,128)} custom-call(f32[6,1,64,64]{3,2,1,0:T(8,128)S(1)} %add_bitcast_fusion.5), custom_call_target="InvertDiagBlocksLowerTriangular" | custom-call | tf_op jit(solution)/shard_map/jvp()/while/body/eval_jaxpr/jit(_solve_triangular)/vmap()/triangular_solve/custom-call.1 | solution.py:70
  266.3 30.1 %custom-call.46 = f32[6,1,64,64]{2,3,1,0:T(8,128)} custom-call(f32[6,1,64,64]{3,2,1,0:T(8,128)S(1)} %add_bitcast_fusion.5), custom_call_target="InvertDiagBlocksLowerTriangular" | custom-call | tf_op jit(solution)/shard_map/jvp()/while/body/eval_jaxpr/jit(_solve_triangular)/vmap()/triangular_solve/custom-call.1 | solution.py:70
  339.2 5.0 fusion.337
  344.2 7.2 multiply_convert_fusion
  351.5 5.7 fusion.338
  357.1 5.6 multiply_reduce_fusion.6
  364.5 4.9 fusion.243
  383.4 137.2 %while.102 = (s32[]{:T(128)}, f32[1,6,128,256]{2,3,1,0:T(8,128)S(1)}, f32[2,1,6,64,128]{4,3,2,1,0:T(8,128)}, f32[2,1,6,64,128]{4,3,0,2,1:T(8,128)}, f32[2,1,6,64...) while((s32[]{:T(128)}, ...), condition=%wide.region_24.26_spmd.clone, body=%wide.region_14.25_spmd.clone.sunk | while | flops 1457530112 | bytes 72648632 | solution.py:84
  389.5 30.9 %custom-call.44 = f32[6,1,64,64]{2,3,1,0:T(8,128)} custom-call(f32[6,1,64,64]{3,2,1,0:T(8,128)} %add_bitcast_fusion.4), custom_call_target="InvertDiagBlocksLowerTriangular" | custom-call | tf_op jit(solution)/shard_map/transpose(jvp())/while/body/eval_jaxpr/jit(_solve_triangular)/vmap()/triangular_solve | solution.py:70
  457.9 30.9 %custom-call.44 = f32[6,1,64,64]{2,3,1,0:T(8,128)} custom-call(f32[6,1,64,64]{3,2,1,0:T(8,128)} %add_bitcast_fusion.4), custom_call_target="InvertDiagBlocksLowerTriangular" | custom-call | tf_op jit(solution)/shard_map/transpose(jvp())/while/body/eval_jaxpr/jit(_solve_triangular)/vmap()/triangular_solve | solution.py:70
  552.9 11.8 all-gather.1
  567.1 8.7 all-gather
  589.2 28.5 %all-gather.48.cloned.1.call-done = bf16[512,2816]{1,0:T(8,128)(2,1)} async-done(((bf16[128,2816]{1,0:T(8,128)(2,1)}), bf16[512,2816]{1,0:T(8,128)(2,1)}) %all-gather.48.cloned.1.call-update) | async-done | bytes 2883600 | tf_op jit(solution)/shard_map/all_gather | solution.py:249
  622.5 23.7 %all-gather.50.cloned.1.call-done = bf16[512,2816]{1,0:T(8,128)(2,1)} async-done(((bf16[128,2816]{1,0:T(8,128)(2,1)}), bf16[512,2816]{1,0:T(8,128)(2,1)}) %all-gather.50.cloned.1.call-update) | async-done | bytes 2883600 | tf_op jit(solution)/shard_map/all_gather | solution.py:250
  651.0 13.2 all-gather.54.cloned.1.call-done
  664.2 28.5 %all-gather.52.cloned.1.call-done = bf16[512,2816]{1,0:T(8,128)(2,1)} async-done(((bf16[128,2816]{1,0:T(8,128)(2,1)}), bf16[512,2816]{1,0:T(8,128)(2,1)}) %all-gather.52.cloned.1.call-update) | async-done | bytes 2883600 | tf_op jit(solution)/shard_map/all_gather | solution.py:243
  703.6 126.9 %all-reduce.40.cloned.1.call-done = (f32[1024]{0:T(1024)}, f32[4,768]{1,0:T(4,128)}, f32[4,768]{1,0:T(4,128)}, f32[4,1536]{1,0:T(4,128)}, f32[1024,6]{0,1:T(8,12...) async-done(((f32[1024]{0:T(1024)}, f32[4,768]{1,0:T(4,128)}, f32[4,768]{1,0:T(4,128)}, f32[4,1536]{1,0:T(4,128)}, ...) | async-done | bytes 107584 | tf_op jit(solution)/shard_map/psum | solution.py:280
  830.5 66.2 %reduce-scatter.11.cloned.1.call-done = f32[256,96]{0,1:T(8,128)} async-done(((f32[256,768]{0,1:T(8,128)}), f32[256,96]{0,1:T(8,128)}) %reduce-scatter.11.cloned.1.call-update) | async-done | bytes 98320 | tf_op jit(solution)/shard_map/reduce_scatter | solution.py:271
  896.7 66.2 %reduce-scatter.9.cloned.1.call-done = f32[256,96]{0,1:T(8,128)} async-done(((f32[256,768]{0,1:T(8,128)}), f32[256,96]{0,1:T(8,128)}) %reduce-scatter.9.cloned.1.call-update) | async-done | bytes 98320 | tf_op jit(solution)/shard_map/reduce_scatter | solution.py:270
  962.9 69.6 %reduce-scatter.17.cloned.1.call-done = f32[384,128]{1,0:T(8,128)} async-done(((f32[384,1024]{1,0:T(8,128)}), f32[384,128]{1,0:T(8,128)}) %reduce-scatter.17.cloned.1.call-update) | async-done | bytes 196624 | tf_op jit(solution)/shard_map/reduce_scatter | solution.py:274
  1032.6 68.6 %reduce-scatter.13.cloned.1.call-done = f32[256,192]{0,1:T(8,128)} async-done(((f32[256,1536]{0,1:T(8,128)}), f32[256,192]{0,1:T(8,128)}) %reduce-scatter.13.cloned.1.call-update) | async-done | bytes 196624 | tf_op jit(solution)/shard_map/reduce_scatter | solution.py:272
  1101.1 68.4 %reduce-scatter.15.cloned.1.call-done = f32[256,192]{0,1:T(8,128)} async-done(((f32[256,1536]{0,1:T(8,128)}), f32[256,192]{0,1:T(8,128)}) %reduce-scatter.15.cloned.1.call-update) | async-done | bytes 196624 | tf_op jit(solution)/shard_map/reduce_scatter | solution.py:273
  1169.6 75.4 %reduce-scatter.19.cloned.1.call-done = f32[256,352]{0,1:T(8,128)} async-done(((f32[256,2816]{0,1:T(8,128)}), f32[256,352]{0,1:T(8,128)}) %reduce-scatter.19.cloned.1.call-update) | async-done | bytes 360464 | tf_op jit(solution)/shard_map/reduce_scatter | solution.py:275
  1245.0 75.5 %reduce-scatter.21.cloned.1.call-done = f32[256,352]{0,1:T(8,128)} async-done(((f32[256,2816]{0,1:T(8,128)}), f32[256,352]{0,1:T(8,128)}) %reduce-scatter.21.cloned.1.call-update) | async-done | bytes 360464 | tf_op jit(solution)/shard_map/reduce_scatter | solution.py:276
  1320.4 76.0 %reduce-scatter.23.cloned.1.call-done = f32[704,128]{1,0:T(8,128)} async-done(((f32[704,1024]{1,0:T(8,128)}), f32[704,128]{1,0:T(8,128)}) %reduce-scatter.23.cloned.1.call-update) | async-done | bytes 360464 | tf_op jit(solution)/shard_map/reduce_scatter | solution.py:277
  (1018 shorter events, 332.3 us)
Async XLA Ops:
  7.2 24.8 %all-gather.26.cloned.1.call-start = ((), (), s32[]{:S(2)}) async-start(), calls=%async_computation.10 | async-start | bytes 1966080 | tf_op jit(solution)/shard_map/all_gather | solution.py:227
  7.9 45.4 %all-gather.22.cloned.1.call-start = ((), (), s32[]{:S(2)}) async-start(), calls=%async_computation.8 | async-start | bytes 1966080 | tf_op jit(solution)/shard_map/all_gather | solution.py:228
  8.7 74.7 %all-gather.24.cloned.1.call-start = ((), (), s32[]{:S(2)}) async-start(), calls=%async_computation.9 | async-start | bytes 3932160 | tf_op jit(solution)/shard_map/all_gather | solution.py:229
  9.4 316.5 %all-gather.28.cloned.1.call-start = ((), (), s32[]{:S(2)}) async-start(), calls=%async_computation.11 | async-start | bytes 3932160 | tf_op jit(solution)/shard_map/all_gather | solution.py:230
  10.0 321.5 %all-gather.30.cloned.1.call-start = ((), (), s32[]{:S(2)}) async-start(), calls=%async_computation.12 | async-start | bytes 3932160 | tf_op jit(solution)/shard_map/all_gather | solution.py:231
  10.6 323.9 %all-gather.32.cloned.1.call-start = ((), (), s32[]{:S(2)}) async-start(), calls=%async_computation.13 | async-start | bytes 7208960 | tf_op jit(solution)/shard_map/all_gather | solution.py:232
  11.2 328.0 %all-gather.34.cloned.1.call-start = ((), (), s32[]{:S(2)}) async-start(), calls=%async_computation.14 | async-start | bytes 7208960 | tf_op jit(solution)/shard_map/all_gather | solution.py:233
  12.0 332.2 %all-gather.36.cloned.1.call-start = ((), (), s32[]{:S(2)}) async-start(), calls=%async_computation.15 | async-start | bytes 7208960 | tf_op jit(solution)/shard_map/all_gather | solution.py:234
  12.8 552.0 %all-gather.38.cloned.1.call-start = ((), (), s32[]{:S(2)}) async-start(), calls=%async_computation.16 | async-start | bytes 1310720 | tf_op jit(solution)/shard_map/all_gather | solution.py:240
  13.9 564.4 %all-gather.42.cloned.1.call-start = ((), (), s32[]{:S(2)}) async-start(), calls=%async_computation.22 | async-start | bytes 1966080 | tf_op jit(solution)/shard_map/all_gather | solution.py:241
  14.9 71.0 %copy-start.163 = (f32[128]{0:T(128)}, f32[128]{0:T(128)S(1)}, u32[]{:S(2)}) copy-start(f32[128]{0:T(128)S(1)} %get-tuple-element.2165) | copy-start | bytes 1540
  14.9 71.0 %copy-start.166 = (f32[128]{0:T(128)}, f32[128]{0:T(128)S(1)}, u32[]{:S(2)}) copy-start(f32[128]{0:T(128)S(1)} %get-tuple-element.2166) | copy-start | bytes 1540
  14.9 71.0 %copy-start.169 = (f32[128]{0:T(128)}, f32[128]{0:T(128)S(1)}, u32[]{:S(2)}) copy-start(f32[128]{0:T(128)S(1)} %get-tuple-element.2167) | copy-start | bytes 1540
  15.0 71.0 %copy-start.106 = (f32[1536]{0:T(1024)}, f32[1536]{0:T(1024)S(1)}, u32[]{:S(2)}) copy-start(f32[1536]{0:T(1024)S(1)} %get-tuple-element.1907) | copy-start | bytes 18436
  15.0 71.0 %copy-start.108 = (f32[1536]{0:T(1024)}, f32[1536]{0:T(1024)S(1)}, u32[]{:S(2)}) copy-start(f32[1536]{0:T(1024)S(1)} %get-tuple-element.1908) | copy-start | bytes 18436
  334.2 244.0 %all-gather.44.cloned.1.call-start = ((), (), s32[]{:S(2)}) async-start(), calls=%async_computation.23 | async-start | bytes 1310720 | tf_op jit(solution)/shard_map/all_gather | solution.py:248
  379.5 202.1 %all-gather.56.cloned.1.call-start = ((), (), s32[]{:S(2)}) async-start(), calls=%async_computation.33 | async-start | bytes 1966080 | tf_op jit(solution)/shard_map/all_gather | solution.py:246
  527.0 58.3 %all-gather.40.cloned.1.call-start = ((), (), s32[]{:S(2)}) async-start(), calls=%async_computation.20 | async-start | bytes 1966080 | tf_op jit(solution)/shard_map/all_gather | solution.py:247
  527.7 61.5 %all-gather.46.cloned.1.call-start = ((), (), s32[]{:S(2)}) async-start(), calls=%async_computation.25 | async-start | bytes 1310720 | tf_op jit(solution)/shard_map/all_gather | solution.py:242
  528.3 89.3 %all-gather.48.cloned.1.call-start = ((), (), s32[]{:S(2)}) async-start(), calls=%async_computation.26 | async-start | bytes 3604480 | tf_op jit(solution)/shard_map/all_gather | solution.py:249
  528.9 117.2 %all-gather.50.cloned.1.call-start = ((), (), s32[]{:S(2)}) async-start(), calls=%async_computation.28 | async-start | bytes 3604480 | tf_op jit(solution)/shard_map/all_gather | solution.py:250
  529.5 134.8 %all-gather.54.cloned.1.call-start = ((), (), s32[]{:S(2)}) async-start(), calls=%async_computation.31 | async-start | bytes 1310720 | tf_op jit(solution)/shard_map/all_gather | solution.py:251
  530.0 162.7 %all-gather.52.cloned.1.call-start = ((), (), s32[]{:S(2)}) async-start(), calls=%async_computation.30 | async-start | bytes 3604480 | tf_op jit(solution)/shard_map/all_gather | solution.py:243
  539.2 291.3 %all-reduce.40.cloned.1.call-start = ((), (), s32[]{:S(2)}) async-start(), calls=%async_computation.34 | async-start | bytes 249856 | tf_op jit(solution)/shard_map/psum | solution.py:280
  564.7 332.1 %reduce-scatter.11.cloned.1.call-start = ((), (), s32[]{:S(2)}) async-start(), calls=%async_computation.18 | async-start | bytes 884736 | tf_op jit(solution)/shard_map/reduce_scatter | solution.py:271
  567.1 395.9 %reduce-scatter.9.cloned.1.call-start = ((), (), s32[]{:S(2)}) async-start(), calls=%async_computation.17 | async-start | bytes 884736 | tf_op jit(solution)/shard_map/reduce_scatter | solution.py:270
  578.2 454.4 %reduce-scatter.17.cloned.1.call-start = ((), (), s32[]{:S(2)}) async-start(), calls=%async_computation.24 | async-start | bytes 1769472 | tf_op jit(solution)/shard_map/reduce_scatter | solution.py:274
  581.5 519.6 %reduce-scatter.13.cloned.1.call-start = ((), (), s32[]{:S(2)}) async-start(), calls=%async_computation.19 | async-start | bytes 1769472 | tf_op jit(solution)/shard_map/reduce_scatter | solution.py:272
  584.9 584.7 %reduce-scatter.15.cloned.1.call-start = ((), (), s32[]{:S(2)}) async-start(), calls=%async_computation.21 | async-start | bytes 1769472 | tf_op jit(solution)/shard_map/reduce_scatter | solution.py:273
  588.6 656.3 %reduce-scatter.19.cloned.1.call-start = ((), (), s32[]{:S(2)}) async-start(), calls=%async_computation.27 | async-start | bytes 3244032 | tf_op jit(solution)/shard_map/reduce_scatter | solution.py:275
  622.4 698.0 %reduce-scatter.21.cloned.1.call-start = ((), (), s32[]{:S(2)}) async-start(), calls=%async_computation.29 | async-start | bytes 3244032 | tf_op jit(solution)/shard_map/reduce_scatter | solution.py:276
  651.0 745.5 %reduce-scatter.23.cloned.1.call-start = ((), (), s32[]{:S(2)}) async-start(), calls=%async_computation.32 | async-start | bytes 3244032 | tf_op jit(solution)/shard_map/reduce_scatter | solution.py:277
  (280 other events, 1449.3 us)
Sparse Core Ops, SparseCore 0:
  9.6 22.3 all-gather.25
  33.5 19.7 all-gather.21
  54.9 28.4 all-gather.23
  84.8 28.6 all-gather.27
  114.9 28.5 all-gather.29
  144.9 43.4 all-gather.31
  190.0 43.4 all-gather.33
  235.1 43.8 all-gather.35
  281.1 17.0 all-gather.37
  334.4 19.6 all-gather.41
  379.7 16.7 all-gather.43
  527.1 19.5 all-gather.55
  548.2 22.1 all-gather.39
  572.4 16.7 all-gather.45
  590.6 27.0 all-gather.47
  619.0 27.0 all-gather.49
  647.5 16.6 all-gather.53
  665.7 27.0 all-gather.51
  700.9 129.5 all-reduce.39
  834.2 62.4 reduce-scatter.10
  900.6 62.2 reduce-scatter.8
  967.0 65.5 reduce-scatter.16
  1036.6 64.5 reduce-scatter.12
  1105.0 64.5 reduce-scatter.14
  1173.7 71.2 reduce-scatter.18
  1248.9 71.4 reduce-scatter.20
  1324.4 72.0 reduce-scatter.22
where the time goes:
time: 1420 us
  waiting for transfers between devices  841 us (59%)
  other arithmetic  256 us (18%)
  matrix products  169 us (12%)
  local copies, waits for them, and re-layouts  109 us (8%)
  blocking collectives  20.5 us (1%)
  between operations  16.6 us (1%)
    another operation x28, other arithmetic, span_step(): jax.scipy.linalg.solve_triangular(system, rhs, lower=True, unit_diagonal=...  185 us
    psum x1, waiting for transfers between devices, body(): lax.psum((small_terms[0], small_terms[1], small_terms[2], small_terms[3],...  127 us
    reduce_scatter x1, waiting for transfers between devices, body(): lax.psum_scatter(own_rows[7], 'rep', scatter_dimension=1, tiled=True)  76 us
    reduce_scatter x1, waiting for transfers between devices, body(): lax.psum_scatter(own_rows[6], 'rep', scatter_dimension=1, tiled=True)  75.5 us
    reduce_scatter x1, waiting for transfers between devices, body(): lax.psum_scatter(own_rows[5], 'rep', scatter_dimension=1, tiled=True)  75.4 us
    reduce_scatter x1, waiting for transfers between devices, body(): lax.psum_scatter(own_rows[4], 'rep', scatter_dimension=1, tiled=True)  69.6 us
    reduce_scatter x1, waiting for transfers between devices, body(): lax.psum_scatter(own_rows[2], 'rep', scatter_dimension=1, tiled=True)  68.6 us
    reduce_scatter x1, waiting for transfers between devices, body(): lax.psum_scatter(own_rows[3], 'rep', scatter_dimension=1, tiled=True)  68.4 us
  transfers between devices with their start and end apart: 27, of which 17 were waited for; matrix products, arithmetic and copies ran while one was open for 35% of the time, Pallas kernels for 0%

commit v1 on v0

--- a/solution.py
+++ b/solution.py
@@ -277,7 +277,7 @@
         lax.psum_scatter(own_rows[7], "rep", scatter_dimension=1, tiled=True),
     )
     small_terms = (mix_small[0], g_gain_mid) + tuple(mix_small[1:])
-    small_final = lax.psum(
+    partial_2 = lax.psum(
         (
             small_terms[0],
             small_terms[1],
@@ -290,8 +290,9 @@
             small_terms[8],
             small_terms[9],
         ),
-        ("shard", "rep"),
-    )
+        "rep",
+    )
+    small_final = lax.psum(partial_2, "shard")
     g_query, g_key, g_value, g_gate_out, g_out, g_ffgate, g_ffup, g_down = large_final
     (
         g_gain_in,

time: 1420 us -> 1470 us (1.035)
  waiting for transfers between devices: 841 us -> 899 us
    psum x1, waiting for transfers between devices: 127 us -> 57.6 us  [body(): lax.psum((small_terms[0], small_terms[1], small_terms[2], small_terms[3],...]
    psum x0 -> x1, waiting for transfers between devices: none -> 24.8 us  [body(): small_final = lax.psum(partial_2, 'shard')]
    all_gather x1, waiting for transfers between devices: 0.02 us -> 18.7 us  [body(): lax.all_gather(mix_pairs[0][0], 'shard', axis=0, tiled=True)]
    all_gather x1, waiting for transfers between devices: 0.02 us -> 18.7 us  [body(): lax.all_gather(mix_pairs[4][1], 'shard', axis=0, tiled=True)]
    all_gather x1, waiting for transfers between devices: 0.02 us -> 18 us  [body(): lax.all_gather(mix_pairs[2][1], 'shard', axis=0, tiled=True)]
    all_gather x1, waiting for transfers between devices: 0.02 us -> 17.4 us  [body(): lax.all_gather(mix_pairs[3][1], 'shard', axis=0, tiled=True)]
    all_gather x1, waiting for transfers between devices: 0.51 us -> 15.3 us  [body(): lax.all_gather(ffn_pairs[0][0], 'shard', axis=0, tiled=True)]
  transfers between devices with their start and end apart: 27 -> 28, of which waited for: 17 -> 23; matrix products, arithmetic and copies ran while one was open for 35% -> 20% of each run, Pallas kernels for 0% -> 0%
where the time goes in v1:
time: 1470 us; the launch traced here: 1460 us
  waiting for transfers between devices  899 us (61%)
  other arithmetic  255 us (17%)
  matrix products  160 us (11%)
  local copies, waits for them, and re-layouts  110 us (7%)
  blocking collectives  17.2 us (1%)
  between operations  16.6 us (1%)
    another operation x28, other arithmetic, span_step(): jax.scipy.linalg.solve_triangular(system, rhs, lower=True, unit_diagonal=...  185 us
    reduce_scatter x1, waiting for transfers between devices, body(): lax.psum_scatter(own_rows[7], 'rep', scatter_dimension=1, tiled=True)  76.4 us
    reduce_scatter x1, waiting for transfers between devices, body(): lax.psum_scatter(own_rows[6], 'rep', scatter_dimension=1, tiled=True)  75.8 us
    reduce_scatter x1, waiting for transfers between devices, body(): lax.psum_scatter(own_rows[5], 'rep', scatter_dimension=1, tiled=True)  75.3 us
    reduce_scatter x1, waiting for transfers between devices, body(): lax.psum_scatter(own_rows[4], 'rep', scatter_dimension=1, tiled=True)  69.6 us
    reduce_scatter x1, waiting for transfers between devices, body(): lax.psum_scatter(own_rows[3], 'rep', scatter_dimension=1, tiled=True)  68.4 us
    reduce_scatter x1, waiting for transfers between devices, body(): lax.psum_scatter(own_rows[2], 'rep', scatter_dimension=1, tiled=True)  68.3 us
    reduce_scatter x1, waiting for transfers between devices, body(): lax.psum_scatter(own_rows[1], 'rep', scatter_dimension=1, tiled=True)  67.2 us
  transfers between devices with their start and end apart: 28, of which 23 were waited for; matrix products, arithmetic and copies ran while one was open for 20% of the time, Pallas kernels for 0%

profile of v1, /device:TPU:0, one launch (start us, length us, event | category | flops | bytes accessed | tf_op | source)
XLA Modules:
  0.0 1462.9 jit_solution(793152101740696060)
XLA Ops:
  20.0 12.0 all-gather.26.cloned.1.call-done
  33.8 19.4 %all-gather.22.cloned.1.call-done = bf16[1024,768]{1,0:T(8,128)(2,1)} async-done(((bf16[256,768]{1,0:T(8,128)(2,1)}), bf16[1024,768]{1,0:T(8,128)(2,1)}) %all-gather.22.cloned.1.call-update) | async-done | bytes 1572880 | tf_op jit(solution)/shard_map/all_gather | solution.py:228
  66.9 16.4 %all-gather.24.cloned.1.call-done = bf16[1024,1536]{1,0:T(8,128)(2,1)} async-done(((bf16[256,1536]{1,0:T(8,128)(2,1)}), bf16[1024,1536]{1,0:T(8,128)(2,1)}) %all-gather.24.cloned.1.call-update) | async-done | bytes 3145744 | tf_op jit(solution)/shard_map/all_gather | solution.py:229
  98.2 119.6 %while.104 = (s32[]{:T(128)}, f32[1,6,128,256]{3,2,1,0:T(8,128)S(1)}, f32[2,1,6,64,256]{4,3,2,1,0:T(8,128)}, f32[2,1,6,64,64]{4,3,2,1,0:T(8,128)}, f32[2,1,6,64,...) while((s32[]{:T(128)}, ...), condition=%wide.region_11.13_spmd.clone.clone, body=%wide.region_9.12_spmd.clone.clone.sunk | while | flops 719999424 | bytes 38057020 | solution.py:84
  106.5 30.2 %custom-call.46 = f32[6,1,64,64]{2,3,1,0:T(8,128)S(1)} custom-call(f32[6,1,64,64]{3,2,1,0:T(8,128)} %add_bitcast_fusion.5), custom_call_target="InvertDiagBlocksLowerTriangular" | custom-call | tf_op jit(solution)/shard_map/jvp()/while/body/eval_jaxpr/jit(_solve_triangular)/vmap()/triangular_solve/custom-call.1 | solution.py:70
  166.1 30.2 %custom-call.46 = f32[6,1,64,64]{2,3,1,0:T(8,128)S(1)} custom-call(f32[6,1,64,64]{3,2,1,0:T(8,128)} %add_bitcast_fusion.5), custom_call_target="InvertDiagBlocksLowerTriangular" | custom-call | tf_op jit(solution)/shard_map/jvp()/while/body/eval_jaxpr/jit(_solve_triangular)/vmap()/triangular_solve/custom-call.1 | solution.py:70
  222.2 83.6 %while.103 = (s32[]{:T(128)}, f32[1,6,128,256]{3,2,1,0:T(8,128)S(1)}, f32[2,1,6,64,256]{4,3,2,1,0:T(8,128)}, f32[2,1,6,64]{3,2,1,0:T(8,128)}, s32[2,1,64]{2,1,0:...) while((s32[]{:T(128)}, ...), condition=%wide.region_5.7_spmd.clone.clone, body=%wide.region_3.6_spmd.clone.clone.sunk | while | flops 719243328 | bytes 16518565 | solution.py:84
  227.8 29.5 %custom-call.45 = f32[6,1,64,64]{2,3,1,0:T(8,128)S(1)} custom-call(f32[6,1,64,64]{3,2,1,0:T(8,128)S(1)} %fusion.510), custom_call_target="InvertDiagBlocksLowerTriangular" | custom-call | tf_op jit(solution)/shard_map/while/body/eval_jaxpr/jit(_solve_triangular)/vmap()/triangular_solve/custom-call.1 | solution.py:70
  269.3 29.5 %custom-call.45 = f32[6,1,64,64]{2,3,1,0:T(8,128)S(1)} custom-call(f32[6,1,64,64]{3,2,1,0:T(8,128)S(1)} %fusion.510), custom_call_target="InvertDiagBlocksLowerTriangular" | custom-call | tf_op jit(solution)/shard_map/while/body/eval_jaxpr/jit(_solve_triangular)/vmap()/triangular_solve/custom-call.1 | solution.py:70
  369.3 133.1 %while.102 = (s32[]{:T(128)}, f32[1,6,128,256]{2,3,1,0:T(8,128)S(1)}, f32[2,1,6,64,128]{4,3,2,1,0:T(8,128)}, f32[2,1,6,64,128]{4,3,0,2,1:T(8,128)}, f32[2,1,6,64...) while((s32[]{:T(128)}, ...), condition=%wide.region_24.26_spmd.clone, body=%wide.region_14.25_spmd.clone.sunk | while | flops 1457530112 | bytes 73533384 | solution.py:84
  375.4 30.9 %custom-call.44 = f32[6,1,64,64]{2,3,1,0:T(8,128)} custom-call(f32[6,1,64,64]{3,2,1,0:T(8,128)} %add_bitcast_fusion.4), custom_call_target="InvertDiagBlocksLowerTriangular" | custom-call | tf_op jit(solution)/shard_map/transpose(jvp())/while/body/eval_jaxpr/jit(_solve_triangular)/vmap()/triangular_solve | solution.py:70
  441.8 30.9 %custom-call.44 = f32[6,1,64,64]{2,3,1,0:T(8,128)} custom-call(f32[6,1,64,64]{3,2,1,0:T(8,128)} %add_bitcast_fusion.4), custom_call_target="InvertDiagBlocksLowerTriangular" | custom-call | tf_op jit(solution)/shard_map/transpose(jvp())/while/body/eval_jaxpr/jit(_solve_triangular)/vmap()/triangular_solve | solution.py:70
  559.0 57.6 %all-reduce.42.cloned.1.call-done = (f32[1024]{0:T(1024)}, f32[4,768]{1,0:T(4,128)}, f32[4,768]{1,0:T(4,128)}, f32[4,1536]{1,0:T(4,128)}, f32[1024,6]{0,1:T(8,12...) async-done(((f32[1024]{0:T(1024)}, f32[4,768]{1,0:T(4,128)}, f32[4,768]{1,0:T(4,128)}, f32[4,1536]{1,0:T(4,128)}, ...) | async-done | bytes 107584 | tf_op jit(solution)/shard_map/psum | solution.py:280
  616.6 18.7 %all-gather.38.cloned.1.call-done = bf16[512,1024]{1,0:T(8,128)(2,1)} async-done(((bf16[128,1024]{1,0:T(8,128)(2,1)}), bf16[512,1024]{1,0:T(8,128)(2,1)}) %all-gather.38.cloned.1.call-update) | async-done | bytes 1048592 | tf_op jit(solution)/shard_map/all_gather | solution.py:240
  647.8 8.8 all-gather.42.cloned.1.call-done
  656.6 18.7 %all-gather.44.cloned.1.call-done = bf16[512,1024]{1,0:T(8,128)(2,1)} async-done(((bf16[128,1024]{1,0:T(8,128)(2,1)}), bf16[512,1024]{1,0:T(8,128)(2,1)}) %all-gather.44.cloned.1.call-update) | async-done | bytes 1048592 | tf_op jit(solution)/shard_map/all_gather | solution.py:248
  678.5 18.0 %all-gather.56.cloned.1.call-done = bf16[1,512,1536]{2,1,0:T(8,128)(2,1)} async-done(((bf16[1,128,1536]{2,1,0:T(8,128)(2,1)}), bf16[1,512,1536]{2,1,0:T(8,128)(2,1)}) %all-gather.56.cloned.1.call-update) | async-done | bytes 1572880 | tf_op jit(solution)/shard_map/all_gather | solution.py:246
  700.2 17.4 %all-gather.40.cloned.1.call-done = bf16[512,1536]{1,0:T(8,128)(2,1)} async-done(((bf16[128,1536]{1,0:T(8,128)(2,1)}), bf16[512,1536]{1,0:T(8,128)(2,1)}) %all-gather.40.cloned.1.call-update) | async-done | bytes 1572880 | tf_op jit(solution)/shard_map/all_gather | solution.py:247
  721.0 15.3 %all-gather.46.cloned.1.call-done = bf16[512,1024]{1,0:T(8,128)(2,1)} async-done(((bf16[128,1024]{1,0:T(8,128)(2,1)}), bf16[512,1024]{1,0:T(8,128)(2,1)}) %all-gather.46.cloned.1.call-update) | async-done | bytes 1048592 | tf_op jit(solution)/shard_map/all_gather | solution.py:242
  736.3 28.5 %all-gather.48.cloned.1.call-done = bf16[512,2816]{1,0:T(8,128)(2,1)} async-done(((bf16[128,2816]{1,0:T(8,128)(2,1)}), bf16[512,2816]{1,0:T(8,128)(2,1)}) %all-gather.48.cloned.1.call-update) | async-done | bytes 2883600 | tf_op jit(solution)/shard_map/all_gather | solution.py:249
  769.6 23.7 %all-gather.50.cloned.1.call-done = bf16[512,2816]{1,0:T(8,128)(2,1)} async-done(((bf16[128,2816]{1,0:T(8,128)(2,1)}), bf16[512,2816]{1,0:T(8,128)(2,1)}) %all-gather.50.cloned.1.call-update) | async-done | bytes 2883600 | tf_op jit(solution)/shard_map/all_gather | solution.py:250
  798.1 13.3 all-gather.54.cloned.1.call-done
  811.4 28.6 %all-gather.52.cloned.1.call-done = bf16[512,2816]{1,0:T(8,128)(2,1)} async-done(((bf16[128,2816]{1,0:T(8,128)(2,1)}), bf16[512,2816]{1,0:T(8,128)(2,1)}) %all-gather.52.cloned.1.call-update) | async-done | bytes 2883600 | tf_op jit(solution)/shard_map/all_gather | solution.py:243
  851.0 24.8 %all-reduce.44.cloned.1.call-done = (f32[1024]{0:T(1024)}, f32[4,768]{1,0:T(4,128)}, f32[4,768]{1,0:T(4,128)}, f32[4,1536]{1,0:T(4,128)}, f32[1024,6]{0,1:T(8,12...) async-done(((f32[1024]{0:T(1024)}, f32[4,768]{1,0:T(4,128)}, f32[4,768]{1,0:T(4,128)}, f32[4,1536]{1,0:T(4,128)}, ...) | async-done | bytes 107584 | tf_op jit(solution)/shard_map/psum | solution.py:295
  875.8 67.2 %reduce-scatter.11.cloned.1.call-done = f32[256,96]{0,1:T(8,128)} async-done(((f32[256,768]{0,1:T(8,128)}), f32[256,96]{0,1:T(8,128)}) %reduce-scatter.11.cloned.1.call-update) | async-done | bytes 98320 | tf_op jit(solution)/shard_map/reduce_scatter | solution.py:271
  943.0 66.2 %reduce-scatter.9.cloned.1.call-done = f32[256,96]{0,1:T(8,128)} async-done(((f32[256,768]{0,1:T(8,128)}), f32[256,96]{0,1:T(8,128)}) %reduce-scatter.9.cloned.1.call-update) | async-done | bytes 98320 | tf_op jit(solution)/shard_map/reduce_scatter | solution.py:270
  1009.2 69.6 %reduce-scatter.17.cloned.1.call-done = f32[384,128]{1,0:T(8,128)} async-done(((f32[384,1024]{1,0:T(8,128)}), f32[384,128]{1,0:T(8,128)}) %reduce-scatter.17.cloned.1.call-update) | async-done | bytes 196624 | tf_op jit(solution)/shard_map/reduce_scatter | solution.py:274
  1078.8 68.3 %reduce-scatter.13.cloned.1.call-done = f32[256,192]{0,1:T(8,128)} async-done(((f32[256,1536]{0,1:T(8,128)}), f32[256,192]{0,1:T(8,128)}) %reduce-scatter.13.cloned.1.call-update) | async-done | bytes 196624 | tf_op jit(solution)/shard_map/reduce_scatter | solution.py:272
  1147.2 68.4 %reduce-scatter.15.cloned.1.call-done = f32[256,192]{0,1:T(8,128)} async-done(((f32[256,1536]{0,1:T(8,128)}), f32[256,192]{0,1:T(8,128)}) %reduce-scatter.15.cloned.1.call-update) | async-done | bytes 196624 | tf_op jit(solution)/shard_map/reduce_scatter | solution.py:273
  1215.5 75.3 %reduce-scatter.19.cloned.1.call-done = f32[256,352]{0,1:T(8,128)} async-done(((f32[256,2816]{0,1:T(8,128)}), f32[256,352]{0,1:T(8,128)}) %reduce-scatter.19.cloned.1.call-update) | async-done | bytes 360464 | tf_op jit(solution)/shard_map/reduce_scatter | solution.py:275
  1290.8 75.8 %reduce-scatter.21.cloned.1.call-done = f32[256,352]{0,1:T(8,128)} async-done(((f32[256,2816]{0,1:T(8,128)}), f32[256,352]{0,1:T(8,128)}) %reduce-scatter.21.cloned.1.call-update) | async-done | bytes 360464 | tf_op jit(solution)/shard_map/reduce_scatter | solution.py:276
  1366.6 76.4 %reduce-scatter.23.cloned.1.call-done = f32[704,128]{1,0:T(8,128)} async-done(((f32[704,1024]{1,0:T(8,128)}), f32[704,128]{1,0:T(8,128)}) %reduce-scatter.23.cloned.1.call-update) | async-done | bytes 360464 | tf_op jit(solution)/shard_map/reduce_scatter | solution.py:277
  (1033 shorter events, 372.9 us)
Async XLA Ops:
  7.2 24.8 %all-gather.26.cloned.1.call-start = ((), (), s32[]{:S(2)}) async-start(), calls=%async_computation.10 | async-start | bytes 1966080 | tf_op jit(solution)/shard_map/all_gather | solution.py:227
  7.9 45.2 %all-gather.22.cloned.1.call-start = ((), (), s32[]{:S(2)}) async-start(), calls=%async_computation.8 | async-start | bytes 1966080 | tf_op jit(solution)/shard_map/all_gather | solution.py:228
  8.7 74.6 %all-gather.24.cloned.1.call-start = ((), (), s32[]{:S(2)}) async-start(), calls=%async_computation.9 | async-start | bytes 3932160 | tf_op jit(solution)/shard_map/all_gather | solution.py:229
  9.4 303.2 %all-gather.28.cloned.1.call-start = ((), (), s32[]{:S(2)}) async-start(), calls=%async_computation.11 | async-start | bytes 3932160 | tf_op jit(solution)/shard_map/all_gather | solution.py:230
  10.0 307.9 %all-gather.30.cloned.1.call-start = ((), (), s32[]{:S(2)}) async-start(), calls=%async_computation.12 | async-start | bytes 3932160 | tf_op jit(solution)/shard_map/all_gather | solution.py:231
  10.6 310.2 %all-gather.32.cloned.1.call-start = ((), (), s32[]{:S(2)}) async-start(), calls=%async_computation.13 | async-start | bytes 7208960 | tf_op jit(solution)/shard_map/all_gather | solution.py:232
  11.2 314.3 %all-gather.34.cloned.1.call-start = ((), (), s32[]{:S(2)}) async-start(), calls=%async_computation.14 | async-start | bytes 7208960 | tf_op jit(solution)/shard_map/all_gather | solution.py:233
  12.0 318.2 %all-gather.36.cloned.1.call-start = ((), (), s32[]{:S(2)}) async-start(), calls=%async_computation.15 | async-start | bytes 7208960 | tf_op jit(solution)/shard_map/all_gather | solution.py:234
  12.8 603.8 %all-reduce.42.cloned.1.call-start = ((), (), s32[]{:S(2)}) async-start(), calls=%async_computation.34 | async-start | bytes 249856 | tf_op jit(solution)/shard_map/psum | solution.py:280
  13.9 71.9 %copy-start.159 = (f32[128]{0:T(128)}, f32[128]{0:T(128)S(1)}, u32[]{:S(2)}) copy-start(f32[128]{0:T(128)S(1)} %get-tuple-element.2175) | copy-start | bytes 1540
  13.9 71.9 %copy-start.162 = (f32[128]{0:T(128)}, f32[128]{0:T(128)S(1)}, u32[]{:S(2)}) copy-start(f32[128]{0:T(128)S(1)} %get-tuple-element.2176) | copy-start | bytes 1540
  13.9 71.9 %copy-start.165 = (f32[128]{0:T(128)}, f32[128]{0:T(128)S(1)}, u32[]{:S(2)}) copy-start(f32[128]{0:T(128)S(1)} %get-tuple-element.2177) | copy-start | bytes 1540
  14.0 71.8 %copy-start.110 = (f32[1536]{0:T(1024)}, f32[1536]{0:T(1024)S(1)}, u32[]{:S(2)}) copy-start(f32[1536]{0:T(1024)S(1)} %get-tuple-element.1907) | copy-start | bytes 18436
  544.0 91.3 %all-gather.38.cloned.1.call-start = ((), (), s32[]{:S(2)}) async-start(), calls=%async_computation.16 | async-start | bytes 1310720 | tf_op jit(solution)/shard_map/all_gather | solution.py:240
  544.6 112.0 %all-gather.42.cloned.1.call-start = ((), (), s32[]{:S(2)}) async-start(), calls=%async_computation.22 | async-start | bytes 1966080 | tf_op jit(solution)/shard_map/all_gather | solution.py:241
  545.3 130.0 %all-gather.44.cloned.1.call-start = ((), (), s32[]{:S(2)}) async-start(), calls=%async_computation.23 | async-start | bytes 1310720 | tf_op jit(solution)/shard_map/all_gather | solution.py:248
  545.9 150.6 %all-gather.56.cloned.1.call-start = ((), (), s32[]{:S(2)}) async-start(), calls=%async_computation.33 | async-start | bytes 1966080 | tf_op jit(solution)/shard_map/all_gather | solution.py:246
  546.7 170.9 %all-gather.40.cloned.1.call-start = ((), (), s32[]{:S(2)}) async-start(), calls=%async_computation.20 | async-start | bytes 1966080 | tf_op jit(solution)/shard_map/all_gather | solution.py:247
  547.2 189.1 %all-gather.46.cloned.1.call-start = ((), (), s32[]{:S(2)}) async-start(), calls=%async_computation.25 | async-start | bytes 1310720 | tf_op jit(solution)/shard_map/all_gather | solution.py:242
  547.8 217.0 %all-gather.48.cloned.1.call-start = ((), (), s32[]{:S(2)}) async-start(), calls=%async_computation.26 | async-start | bytes 3604480 | tf_op jit(solution)/shard_map/all_gather | solution.py:249
  548.4 244.8 %all-gather.50.cloned.1.call-start = ((), (), s32[]{:S(2)}) async-start(), calls=%async_computation.28 | async-start | bytes 3604480 | tf_op jit(solution)/shard_map/all_gather | solution.py:250
  549.0 262.4 %all-gather.54.cloned.1.call-start = ((), (), s32[]{:S(2)}) async-start(), calls=%async_computation.31 | async-start | bytes 1310720 | tf_op jit(solution)/shard_map/all_gather | solution.py:251
  549.6 290.4 %all-gather.52.cloned.1.call-start = ((), (), s32[]{:S(2)}) async-start(), calls=%async_computation.30 | async-start | bytes 3604480 | tf_op jit(solution)/shard_map/all_gather | solution.py:243
  550.3 325.5 %all-reduce.44.cloned.1.call-start = ((), (), s32[]{:S(2)}) async-start(), calls=%async_computation.35 | async-start | bytes 249856 | tf_op jit(solution)/shard_map/psum | solution.py:295
  616.6 326.5 %reduce-scatter.11.cloned.1.call-start = ((), (), s32[]{:S(2)}) async-start(), calls=%async_computation.18 | async-start | bytes 884736 | tf_op jit(solution)/shard_map/reduce_scatter | solution.py:271
  637.7 371.5 %reduce-scatter.9.cloned.1.call-start = ((), (), s32[]{:S(2)}) async-start(), calls=%async_computation.17 | async-start | bytes 884736 | tf_op jit(solution)/shard_map/reduce_scatter | solution.py:270
  647.7 431.1 %reduce-scatter.17.cloned.1.call-start = ((), (), s32[]{:S(2)}) async-start(), calls=%async_computation.24 | async-start | bytes 1769472 | tf_op jit(solution)/shard_map/reduce_scatter | solution.py:274
  678.4 468.7 %reduce-scatter.13.cloned.1.call-start = ((), (), s32[]{:S(2)}) async-start(), calls=%async_computation.19 | async-start | bytes 1769472 | tf_op jit(solution)/shard_map/reduce_scatter | solution.py:272
  699.9 515.6 %reduce-scatter.15.cloned.1.call-start = ((), (), s32[]{:S(2)}) async-start(), calls=%async_computation.21 | async-start | bytes 1769472 | tf_op jit(solution)/shard_map/reduce_scatter | solution.py:273
  720.9 569.9 %reduce-scatter.19.cloned.1.call-start = ((), (), s32[]{:S(2)}) async-start(), calls=%async_computation.27 | async-start | bytes 3244032 | tf_op jit(solution)/shard_map/reduce_scatter | solution.py:275
  769.5 597.1 %reduce-scatter.21.cloned.1.call-start = ((), (), s32[]{:S(2)}) async-start(), calls=%async_computation.29 | async-start | bytes 3244032 | tf_op jit(solution)/shard_map/reduce_scatter | solution.py:276
  798.0 645.0 %reduce-scatter.23.cloned.1.call-start = ((), (), s32[]{:S(2)}) async-start(), calls=%async_computation.32 | async-start | bytes 3244032 | tf_op jit(solution)/shard_map/reduce_scatter | solution.py:277
  (287 other events, 1551.9 us)
Sparse Core Ops, SparseCore 0:
  9.6 22.3 all-gather.25
  33.5 19.6 all-gather.21
  54.8 28.4 all-gather.23
  84.7 28.5 all-gather.27
  114.7 28.5 all-gather.29
  144.7 43.8 all-gather.31
  190.2 43.6 all-gather.33
  235.4 43.7 all-gather.35
  544.1 72.3 all-reduce.41
  618.5 16.7 all-gather.37
  636.9 19.6 all-gather.41
  658.6 16.6 all-gather.43
  676.9 19.6 all-gather.55
  697.9 19.6 all-gather.39
  719.6 16.6 all-gather.45
  737.7 27.0 all-gather.47
  766.2 27.0 all-gather.49
  794.7 16.6 all-gather.53
  812.9 27.0 all-gather.51
  842.9 32.9 all-reduce.43
  879.7 63.2 reduce-scatter.10
  946.9 62.2 reduce-scatter.8
  1013.2 65.5 reduce-scatter.16
  1082.7 64.4 reduce-scatter.12
  1151.1 64.3 reduce-scatter.14
  1219.5 71.2 reduce-scatter.18
  1294.8 71.7 reduce-scatter.20
  1370.8 72.2 reduce-scatter.22
